TPU v7x, 32 devices: a whole 2x2x4 slice. The times are simulated.
32 devices in a mesh: vol: 8 (over z, x), rep: 4 (over y, core).
Axes of the slice: x: 2, y: 2, z: 4, core: 2. Of those that a mesh axis runs over, the one named last changes fastest.
Arguments:
- cutouts: bfloat16 [4, 256, 4096], P('rep', 'vol'), may hold values from -6 to 6
- counts: int32 [4, 8], P('rep', 'vol'), may hold values from 1 to 32, as said below
- partner: int32 [4, 128], P('rep'), may hold values from 0 to 127, as said below
- w_stem: bfloat16 [64, 128], replicated, may hold values from -0.75 to 0.75
- w_mix: bfloat16 [128, 128], replicated, may hold values from -0.5 to 0.5
- w_out: bfloat16 [128, 128], replicated, may hold values from -0.5 to 0.5
- w_proj: bfloat16 [128, 64], replicated, may hold values from -0.5 to 0.5
Outputs:
- upd_stem: float32 [64, 128], replicated
- upd_mix: float32 [128, 128], replicated
- upd_out: float32 [128, 128], replicated
- upd_proj: float32 [128, 64], replicated
- node_loss: float32 [4, 8, 16], P('rep', 'vol')
Inputs may be any that keep to these rules, and one draw needn't show every extreme that they name: `counts`: each row sums to 128, and its largest entry is exactly 32. Each row pairs the nodes of a group: partner[r, partner[r, g]] = g and partner[r, g] != g.
All inputs are finite; a program needn't handle non-finite values.
Results may differ from a plain program's by a relative error of at most 0.0035.
Values may be sent and summed in bfloat16 or wider, within the bound.
No kernel may reach another device: no remote copies, remote signals or barrier semaphores. Data moves between devices by JAX's collectives and lax.ppermute only.
A program may use at most 64 MiB of HBM per device.

v0:
```python
import jax
import jax.numpy as jnp
from jax import lax
from jax.sharding import PartitionSpec as P

logit_divisor_factor = 0.2
norm_eps = 1e-06
rms_eps = 1e-06


def prefix(part, axis, combine, identity):
    place = lax.axis_index(axis)
    gathered = lax.all_gather(part, axis)
    state = jnp.zeros_like(part) + jnp.asarray(identity, part.dtype)

    def one(lap, state):
        return combine(state, lax.dynamic_index_in_dim(gathered, lap, 0, False))

    return lax.fori_loop(0, place, one, state)


def first_dot(left, right):
    return lax.dot_general(
        left, right, (((0,), (0,)), ((), ())), preferred_element_type=jnp.float32
    )


def concluding_matrix_multiply(left, right):
    return lax.dot_general(
        left, right, (((1,), (1,)), ((), ())), preferred_element_type=jnp.float32
    )


def silu_slope(value):
    sigma = jax.nn.sigmoid(value)
    return sigma * (1.0 + value * (1.0 - sigma))


def encode(cutout_rows, w_stem, w_mix, w_out, w_proj):
    number = cutout_rows.shape[0]
    patches = cutout_rows.reshape(-1, w_stem.shape[0])
    per_cutout = patches.shape[0] // number
    pre_stem = jnp.dot(patches, w_stem, preferred_element_type=jnp.float32)
    hidden = jax.nn.silu(pre_stem).astype(jnp.bfloat16)
    pre_mix = jnp.dot(hidden, w_mix, preferred_element_type=jnp.float32)
    mixed = jax.nn.silu(pre_mix).astype(jnp.bfloat16)
    summed = hidden.astype(jnp.float32) + jnp.dot(mixed, w_out, preferred_element_type=jnp.float32)
    pooled = jnp.mean(summed.reshape(number, per_cutout, -1), axis=1).astype(jnp.bfloat16)
    raw_embed = jnp.dot(pooled, w_proj, preferred_element_type=jnp.float32)
    inv_norm = lax.rsqrt(jnp.sum(raw_embed * raw_embed, axis=1, keepdims=True) + norm_eps)
    unit_embed = raw_embed * inv_norm
    return (unit_embed, (patches, pre_stem, hidden, pre_mix, mixed, pooled, unit_embed, inv_norm))


def backward(feature_vector_derivative, saved, w_mix, w_out, w_proj):
    patches, pre_stem, hidden, pre_mix, mixed, pooled, unit_embed, inv_norm = saved
    number = pooled.shape[0]
    per_cutout = patches.shape[0] // number
    channels = hidden.shape[1]
    radial = jnp.sum(unit_embed * feature_vector_derivative, axis=1, keepdims=True)
    grad_raw = (inv_norm * (feature_vector_derivative - unit_embed * radial)).astype(jnp.bfloat16)
    grad_proj = first_dot(pooled, grad_raw)
    grad_pool = (concluding_matrix_multiply(grad_raw, w_proj) / per_cutout).astype(jnp.bfloat16)
    mixed_sum = jnp.sum(mixed.reshape(number, per_cutout, channels), axis=1, dtype=jnp.float32)
    grad_out = lax.dot_general(
        mixed_sum,
        grad_pool.astype(jnp.float32),
        (((0,), (0,)), ((), ())),
        precision=lax.Precision.HIGHEST,
        preferred_element_type=jnp.float32,
    )
    grad_mixed = concluding_matrix_multiply(grad_pool, w_out)
    mix_slope = silu_slope(pre_mix).reshape(number, per_cutout, channels)
    grad_pre_mix = (grad_mixed[:, None, :] * mix_slope).reshape(-1, channels).astype(jnp.bfloat16)
    grad_mix = first_dot(hidden, grad_pre_mix)
    spread_pool = jnp.broadcast_to(
        grad_pool.astype(jnp.float32)[:, None, :], (number, per_cutout, channels)
    ).reshape(-1, channels)
    grad_hidden = spread_pool + concluding_matrix_multiply(grad_pre_mix, w_mix)
    grad_pre_stem = (grad_hidden * silu_slope(pre_stem)).astype(jnp.bfloat16)
    grad_stem = first_dot(patches, grad_pre_stem)
    return (grad_stem, grad_mix, grad_out, grad_proj)


def contrast(anchor_feature_matrix, whole_feature_matrix, self_pos, pair_pos):
    cosine_affinity_matrix = (
        concluding_matrix_multiply(anchor_feature_matrix, whole_feature_matrix)
        / logit_divisor_factor
    )
    columns = lax.broadcasted_iota(jnp.int32, cosine_affinity_matrix.shape, 1)
    exp_scores = jnp.where(columns == self_pos[:, None], 0.0, jnp.exp(cosine_affinity_matrix))
    log_total = jnp.log(jnp.sum(exp_scores, axis=1))
    companion_feature_vector = jnp.take(whole_feature_matrix, pair_pos, axis=0).astype(jnp.float32)
    positive_couple_affinity = (
        jnp.sum(anchor_feature_matrix.astype(jnp.float32) * companion_feature_vector, axis=1)
        / logit_divisor_factor
    )
    return (exp_scores, log_total, companion_feature_vector, log_total - positive_couple_affinity)


def add_counts(earlier, later):
    return earlier + later


def locate(recv_ids, node_rank, slot_index):
    matches = recv_ids[None, :] == node_rank[:, None]
    from_slot = jnp.sum(jnp.where(matches, slot_index[None, :], 0), axis=1)
    return (matches, from_slot)


def on_device(cutouts, counts, partner, w_stem, w_mix, w_out, w_proj):
    vol_size = lax.axis_size("vol")
    vol_index = lax.axis_index("vol")
    max_nodes = cutouts.shape[1]
    node_dev = partner.shape[1] // vol_size
    capacity = (max_nodes + vol_size - 1) // vol_size
    own_cutouts = cutouts[0]
    own_count = counts[0, 0]
    offset = prefix(counts, "vol", add_counts, jnp.zeros_like(counts))[0, 0]
    slot_index = jnp.arange(vol_size * capacity, dtype=jnp.int32)
    target = slot_index // capacity
    first_rank = (offset - target + vol_size - 1) // vol_size
    slot_rank = first_rank + slot_index % capacity
    local_slot = slot_rank * vol_size + target - offset
    is_live = local_slot < own_count
    local_safe = jnp.clip(local_slot, 0, max_nodes - 1)
    send_ids = jnp.where(is_live, slot_rank, -1).astype(jnp.int32)
    node_rank = jnp.arange(node_dev, dtype=jnp.int32)
    packed = jnp.where(
        is_live[:, None], jnp.take(own_cutouts, local_safe, axis=0), jnp.zeros((), jnp.bfloat16)
    )
    arrived, recv_ids = (
        lax.all_to_all(packed, "vol", split_axis=0, concat_axis=0, tiled=True),
        lax.all_to_all(send_ids, "vol", split_axis=0, concat_axis=0, tiled=True),
    )
    matches, from_slot = locate(recv_ids, node_rank, slot_index)
    unit_embed, saved = encode(jnp.take(arrived, from_slot, axis=0), w_stem, w_mix, w_out, w_proj)
    anchor_feature_matrix = unit_embed.astype(jnp.bfloat16)
    whole_feature_matrix = lax.all_gather(anchor_feature_matrix, "vol", axis=0, tiled=True)
    self_pos = vol_index * node_dev + node_rank
    node_global = node_rank * vol_size + vol_index
    pair_global = jnp.take(partner[0], node_global)
    pair_pos = pair_global % vol_size * node_dev + pair_global // vol_size
    exp_scores, log_total, companion_feature_vector, node_loss = contrast(
        anchor_feature_matrix, whole_feature_matrix, self_pos, pair_pos
    )
    row_weight = (exp_scores * jnp.exp(-log_total)[:, None]).astype(jnp.bfloat16)
    horizontal_objective_term = jnp.dot(
        row_weight, whole_feature_matrix, preferred_element_type=jnp.float32
    )
    all_totals = lax.all_gather(log_total, "vol", axis=0, tiled=True)
    column_weight = (exp_scores * jnp.exp(-all_totals)[None, :]).astype(jnp.bfloat16)
    vertical_objective_term = jnp.dot(
        column_weight, whole_feature_matrix, preferred_element_type=jnp.float32
    )
    feature_vector_derivative = (
        horizontal_objective_term + vertical_objective_term - 2.0 * companion_feature_vector
    ) / logit_divisor_factor
    grads = backward(feature_vector_derivative, saved, w_mix, w_out, w_proj)
    grad_totals = lax.psum((grads[0], grads[1], grads[2], grads[3]), ("vol", "rep"))
    updates = [
        summed_grad * lax.rsqrt(jnp.mean(summed_grad * summed_grad) + rms_eps)
        for summed_grad in grad_totals
    ]
    return (updates[0], updates[1], updates[2], updates[3], node_loss[None, None, :])


def solution(mesh):
    in_specs = (P("rep", "vol", None), P("rep", "vol"), P("rep", None), P(), P(), P(), P())
    out_specs = (P(), P(), P(), P(), P("rep", "vol", None))
    return jax.shard_map(
        on_device, mesh=mesh, in_specs=in_specs, out_specs=out_specs, check_vma=False
    )
```

profile of v0, /device:TPU:0, one launch (start us, length us, event | category | flops | bytes accessed | tf_op | source)
XLA Modules:
  0.0 372.9 jit_solution(8634578186639433932)
XLA Ops:
  8.5 0.7 bitcast_dynamic-update-slice_fusion
  9.2 13.1 %all-reduce = s32[8]{0:T(128)S(1)} all-reduce(s32[8]{0:T(128)S(1)} %bitcast_dynamic-update-slice_fusion), channel_id=2, replica_groups=mesh['vol'=8,'rep'=4] {'vol'}, use_global_device_ids=true, to_apply=%add | all-reduce | flops 8 | bytes 64
  22.9 11.2 %all-to-all-start = ((s32[8,4,1]{1,2,0:T(1,128)}), s32[8,4,1]{1,2,0:T(1,128)S(1)}, u32[]{:S(2)}, u32[]{:S(2)}) async-start(s32[8,4,1]{1,2,0:T(1,128)} %compare_select_fusion), calls=%async_computation | async-start | bytes 8192 | tf_op jit(solution)/shard_map/all_to_all | solution.py:134
  34.2 0.6 copy-done.1
  34.8 0.7 gather_fusion.2
  35.6 0.7 gather_fusion
  36.5 0.9 select_select_fusion
  38.0 2.5 all-to-all-done
  40.6 3.5 all-to-all-start.1
  44.6 0.7 reduce.3
  45.7 6.6 %all-to-all-done.1 = bf16[8,4,4096]{2,1,0:T(4,128)(2,1)S(1)} async-done(((bf16[8,4,4096]{2,1,0:T(4,128)(2,1)}), bf16[8,4,4096]{2,1,0:T(4,128)(2,1)S(1)}, u32[]{:S(2)}, u32[]{:S(2)}) %all-to-all-start.1) | async-done | bytes 262176 | tf_op jit(solution)/shard_map/all_to_all | solution.py:133
  53.7 0.9 multiply_convert_fusion.1
  56.4 30.6 %all_gather.14 = bf16[128,64]{1,0:T(8,128)(2,1)S(1)} all-gather(bf16[16,64]{1,0:T(8,128)(2,1)S(1)} %multiply_convert_fusion.6), channel_id=1, replica_groups=mesh['vol'=8,'rep'=4] {'vol'}, dimensions={0}, use_global_device_ids=true | all-gather | bytes 18432 | tf_op jit(solution)/shard_map/all_gather | solution.py:139
  88.6 18.7 %all-reduce.1 = f32[128]{0:T(128)S(1)} all-reduce(f32[128]{0:T(128)S(1)} %get-tuple-element.60), channel_id=1, replica_groups=mesh['vol'=8,'rep'=4] {'vol'}, use_global_device_ids=true, to_apply=%add.1 | all-reduce | flops 128 | bytes 1024
  108.0 0.8 fusion.31
  109.2 0.9 fusion.51
  110.1 1.1 fusion.2
  111.3 0.9 fusion.52
  112.2 116.4 %all-reduce.7.cloned.1.call-done = (f32[64,128]{1,0:T(8,128)}, f32[128,64]{0,1:T(8,128)}) async-done(((f32[64,128]{1,0:T(8,128)}, f32[128,64]{0,1:T(8,128)}), (f32[64,128]{1,0:T(8,128)}, f32[128,64]{0,1:T(8,128)})) %all-reduce.7.cloned.1.call-update) | async-done | bytes 65552 | tf_op jit(solution)/shard_map/psum | solution.py:160
  228.6 1.4 multiply_reduce_fusion.2
  233.4 127.7 %all-reduce.9.cloned.1.call-done = (f32[128,128]{1,0:T(8,128)}, f32[128,128]{1,0:T(8,128)}) async-done(((f32[128,128]{1,0:T(8,128)}, f32[128,128]{1,0:T(8,128)}), (f32[128,128]{1,0:T(8,128)}, f32[128,128]{1,0:T(8,128)})) %all-reduce.9.cloned.1.call-update) | async-done | bytes 131088 | tf_op jit(solution)/shard_map/psum | solution.py:160
  361.1 1.5 multiply_reduce_fusion
  364.6 0.6 broadcast_multiply_fusion.1
  365.4 0.6 broadcast_multiply_fusion
  (72 shorter events, 11.0 us)
Async XLA Ops:
  7.2 28.5 %copy-start = (bf16[1,32,4096]{2,1,0:T(8,128)(2,1)S(1)}, bf16[1,32,4096]{2,1,0:T(8,128)(2,1)}, u32[]{:S(2)}) copy-start(bf16[1,32,4096]{2,1,0:T(8,128)(2,1)} %param.9) | copy-start | bytes 786436
  7.2 0.7 copy-start.10
  22.9 17.6 %all-to-all-start = ((s32[8,4,1]{1,2,0:T(1,128)}), s32[8,4,1]{1,2,0:T(1,128)S(1)}, u32[]{:S(2)}, u32[]{:S(2)}) async-start(s32[8,4,1]{1,2,0:T(1,128)} %compare_select_fusion), calls=%async_computation | async-start | bytes 8192 | tf_op jit(solution)/shard_map/all_to_all | solution.py:134
  34.2 0.7 copy-start.1
  40.6 11.7 %all-to-all-start.1 = ((bf16[8,4,4096]{2,1,0:T(4,128)(2,1)}), bf16[8,4,4096]{2,1,0:T(4,128)(2,1)S(1)}, u32[]{:S(2)}, u32[]{:S(2)}) async-start(bf16[8,4,4096]{2,1,0:T(4,128)(2,1)} %select_select_fusion), calls=%async_computation.1 | async-start | bytes 524288 | tf_op jit(solution)/shard_map/all_to_all | solution.py:133
  44.1 184.6 %all-reduce.7.cloned.1.call-start = ((), (), s32[]{:S(2)}) async-start(), calls=%async_computation.2 | async-start | bytes 131072 | tf_op jit(solution)/shard_map/psum | solution.py:160
  53.0 0.7 copy-start.9
  53.7 0.9 copy-start.8
  54.6 0.8 copy-start.7
  55.4 0.7 copy-start.6
  111.2 249.8 %all-reduce.9.cloned.1.call-start = ((), (), s32[]{:S(2)}) async-start(), calls=%async_computation.3 | async-start | bytes 262144 | tf_op jit(solution)/shard_map/psum | solution.py:160
  228.6 2.1 copy-start.5
  232.0 0.8 copy-start.4
  361.1 2.2 copy-start.3
  364.6 0.8 copy-start.2
Sparse Core Ops, SparseCore 0:
  111.4 117.2 all-reduce.6
  234.9 126.0 all-reduce.8
where the time goes:
time: 374 us; the launch traced here: 373 us
  waiting for transfers between devices  253 us (68%)
  blocking collectives  62.4 us (17%)
  between operations  18.4 us (5%)
  starting transfers between devices  14.8 us (4%)
  other arithmetic  10.2 us (3%)
  local copies, waits for them, and re-layouts  7.41 us (2%)
  matrix products  6.33 us (2%)
    psum x2, waiting for transfers between devices, on_device(): lax.psum((grads[0], grads[1], grads[2], grads[3]), ('vol', 'rep'))  244 us
    unnamed x2, blocking collectives  31.8 us
    all_gather x1, blocking collectives, on_device(): lax.all_gather(anchor_feature_matrix, 'vol', axis=0, tiled=True)  30.6 us
    all_to_all x1, starting transfers between devices, on_device(): lax.all_to_all(send_ids, 'vol', split_axis=0, concat_axis=0, tiled=True)  11.2 us
  transfers between devices with their start and end apart: 4, of which 4 were waited for; matrix products, arithmetic and copies ran while one was open for 2% of the time, Pallas kernels for 0%

commit v1 on v0

--- a/solution.py
+++ b/solution.py
@@ -157,7 +157,9 @@
         horizontal_objective_term + vertical_objective_term - 2.0 * companion_feature_vector
     ) / logit_divisor_factor
     grads = backward(feature_vector_derivative, saved, w_mix, w_out, w_proj)
-    grad_totals = lax.psum((grads[0], grads[1], grads[2], grads[3]), ("vol", "rep"))
+    grad_totals = (grads[0], grads[1], grads[2], grads[3])
+    for over in ("rep", "vol"):
+        grad_totals = lax.psum(grad_totals, over)
     updates = [
         summed_grad * lax.rsqrt(jnp.mean(summed_grad * summed_grad) + rms_eps)
         for summed_grad in grad_totals

time: 374 us -> 334 us (0.89)
  waiting for transfers between devices: 253 us -> 214 us
    psum x2 -> x4, waiting for transfers between devices: 244 us -> 205 us  [on_device(): grad_totals = lax.psum(grad_totals, over)]
  transfers between devices with their start and end apart: 4 -> 6, of which waited for: 4 -> 6; matrix products, arithmetic and copies ran while one was open for 2% -> 2% of each run, Pallas kernels for 0% -> 0%
where the time goes in v1:
time: 334 us
  waiting for transfers between devices  214 us (64%)
  blocking collectives  62.4 us (19%)
  between operations  18.2 us (5%)
  starting transfers between devices  14.9 us (4%)
  other arithmetic  10.2 us (3%)
  local copies, waits for them, and re-layouts  7.41 us (2%)
  matrix products  6.33 us (2%)
    psum x4, waiting for transfers between devices, on_device(): grad_totals = lax.psum(grad_totals, over)  205 us
    unnamed x2, blocking collectives  31.8 us
    all_gather x1, blocking collectives, on_device(): lax.all_gather(anchor_feature_matrix, 'vol', axis=0, tiled=True)  30.6 us
    all_to_all x1, starting transfers between devices, on_device(): lax.all_to_all(send_ids, 'vol', split_axis=0, concat_axis=0, tiled=True)  11.2 us
  transfers between devices with their start and end apart: 6, of which 6 were waited for; matrix products, arithmetic and copies ran while one was open for 2% of the time, Pallas kernels for 0%

profile of v1, /device:TPU:0, one launch (start us, length us, event | category | flops | bytes accessed | tf_op | source)
XLA Modules:
  0.0 333.7 jit_solution(293185939644723265)
XLA Ops:
  8.5 0.7 bitcast_dynamic-update-slice_fusion
  9.2 13.1 %all-reduce = s32[8]{0:T(128)S(1)} all-reduce(s32[8]{0:T(128)S(1)} %bitcast_dynamic-update-slice_fusion), channel_id=2, replica_groups=mesh['vol'=8,'rep'=4] {'vol'}, use_global_device_ids=true, to_apply=%add | all-reduce | flops 8 | bytes 64
  22.9 11.2 %all-to-all-start = ((s32[8,4,1]{1,2,0:T(1,128)}), s32[8,4,1]{1,2,0:T(1,128)S(1)}, u32[]{:S(2)}, u32[]{:S(2)}) async-start(s32[8,4,1]{1,2,0:T(1,128)} %compare_select_fusion), calls=%async_computation | async-start | bytes 8192 | tf_op jit(solution)/shard_map/all_to_all | solution.py:134
  34.2 0.6 copy-done.1
  34.8 0.7 gather_fusion.2
  35.6 0.7 gather_fusion
  36.5 0.9 select_select_fusion
  38.0 2.5 all-to-all-done
  40.6 3.5 %all-to-all-start.1 = ((bf16[8,4,4096]{2,1,0:T(4,128)(2,1)}), bf16[8,4,4096]{2,1,0:T(4,128)(2,1)S(1)}, u32[]{:S(2)}, u32[]{:S(2)}) async-start(bf16[8,4,4096]{2,1,0:T(4,128)(2,1)} %select_select_fusion), calls=%async_computation.1 | async-start | bytes 524288 | tf_op jit(solution)/shard_map/all_to_all | solution.py:133
  44.6 0.7 reduce.3
  45.7 6.6 %all-to-all-done.1 = bf16[8,4,4096]{2,1,0:T(4,128)(2,1)S(1)} async-done(((bf16[8,4,4096]{2,1,0:T(4,128)(2,1)}), bf16[8,4,4096]{2,1,0:T(4,128)(2,1)S(1)}, u32[]{:S(2)}, u32[]{:S(2)}) %all-to-all-start.1) | async-done | bytes 262176 | tf_op jit(solution)/shard_map/all_to_all | solution.py:133
  53.7 0.9 multiply_convert_fusion.1
  56.4 30.6 %all_gather.14 = bf16[128,64]{1,0:T(8,128)(2,1)S(1)} all-gather(bf16[16,64]{1,0:T(8,128)(2,1)S(1)} %multiply_convert_fusion.6), channel_id=1, replica_groups=mesh['vol'=8,'rep'=4] {'vol'}, dimensions={0}, use_global_device_ids=true | all-gather | bytes 18432 | tf_op jit(solution)/shard_map/all_gather | solution.py:139
  88.6 18.7 %all-reduce.1 = f32[128]{0:T(128)S(1)} all-reduce(f32[128]{0:T(128)S(1)} %get-tuple-element.64), channel_id=1, replica_groups=mesh['vol'=8,'rep'=4] {'vol'}, use_global_device_ids=true, to_apply=%add.1 | all-reduce | flops 128 | bytes 1024
  108.0 0.8 fusion.31
  109.2 0.9 fusion.51
  110.1 1.1 fusion.2
  111.3 0.9 fusion.52
  112.2 28.0 %all-reduce.15.cloned.1.call-done = (f32[64,128]{1,0:T(8,128)}, f32[128,64]{0,1:T(8,128)}) async-done(((f32[64,128]{1,0:T(8,128)}, f32[128,64]{0,1:T(8,128)}), (f32[64,128]{1,0:T(8,128)}, f32[128,64]{0,1:T(8,128)})) %all-reduce.15.cloned.1.call-update) | async-done | bytes 65552 | tf_op jit(solution)/shard_map/psum | solution.py:162
  140.3 34.7 %all-reduce.17.cloned.1.call-done = (f32[128,128]{1,0:T(8,128)}, f32[128,128]{1,0:T(8,128)}) async-done(((f32[128,128]{1,0:T(8,128)}, f32[128,128]{1,0:T(8,128)}), (f32[128,128]{1,0:T(8,128)}, f32[128,128]{1,0:T(8,128)})) %all-reduce.17.cloned.1.call-update) | async-done | bytes 131088 | tf_op jit(solution)/shard_map/psum | solution.py:162
  175.1 73.0 %all-reduce.11.cloned.1.call-done = (f32[64,128]{1,0:T(8,128)}, f32[128,64]{0,1:T(8,128)}) async-done(((f32[64,128]{1,0:T(8,128)}, f32[128,64]{0,1:T(8,128)}), (f32[64,128]{1,0:T(8,128)}, f32[128,64]{0,1:T(8,128)})) %all-reduce.11.cloned.1.call-update) | async-done | bytes 65552 | tf_op jit(solution)/shard_map/psum | solution.py:162
  248.1 1.4 multiply_reduce_fusion.2
  252.9 69.3 %all-reduce.13.cloned.1.call-done = (f32[128,128]{1,0:T(8,128)}, f32[128,128]{1,0:T(8,128)}) async-done(((f32[128,128]{1,0:T(8,128)}, f32[128,128]{1,0:T(8,128)}), (f32[128,128]{1,0:T(8,128)}, f32[128,128]{1,0:T(8,128)})) %all-reduce.13.cloned.1.call-update) | async-done | bytes 131088 | tf_op jit(solution)/shard_map/psum | solution.py:162
  322.1 1.5 multiply_reduce_fusion
  (78 shorter events, 12.4 us)
Async XLA Ops:
  7.2 28.5 %copy-start = (bf16[1,32,4096]{2,1,0:T(8,128)(2,1)S(1)}, bf16[1,32,4096]{2,1,0:T(8,128)(2,1)}, u32[]{:S(2)}) copy-start(bf16[1,32,4096]{2,1,0:T(8,128)(2,1)} %param.9) | copy-start | bytes 786436
  7.2 0.7 copy-start.10
  22.9 17.6 %all-to-all-start = ((s32[8,4,1]{1,2,0:T(1,128)}), s32[8,4,1]{1,2,0:T(1,128)S(1)}, u32[]{:S(2)}, u32[]{:S(2)}) async-start(s32[8,4,1]{1,2,0:T(1,128)} %compare_select_fusion), calls=%async_computation | async-start | bytes 8192 | tf_op jit(solution)/shard_map/all_to_all | solution.py:134
  34.2 0.7 copy-start.1
  40.6 11.7 %all-to-all-start.1 = ((bf16[8,4,4096]{2,1,0:T(4,128)(2,1)}), bf16[8,4,4096]{2,1,0:T(4,128)(2,1)S(1)}, u32[]{:S(2)}, u32[]{:S(2)}) async-start(bf16[8,4,4096]{2,1,0:T(4,128)(2,1)} %select_select_fusion), calls=%async_computation.1 | async-start | bytes 524288 | tf_op jit(solution)/shard_map/all_to_all | solution.py:133
  44.1 96.2 %all-reduce.15.cloned.1.call-start = ((), (), s32[]{:S(2)}) async-start(), calls=%async_computation.4 | async-start | bytes 131072 | tf_op jit(solution)/shard_map/psum | solution.py:162
  53.0 0.7 copy-start.9
  53.7 0.9 copy-start.8
  54.6 0.8 copy-start.7
  55.4 0.7 copy-start.6
  111.2 63.8 %all-reduce.17.cloned.1.call-start = ((), (), s32[]{:S(2)}) async-start(), calls=%async_computation.5 | async-start | bytes 262144 | tf_op jit(solution)/shard_map/psum | solution.py:162
  112.2 135.9 %all-reduce.11.cloned.1.call-start = ((), (), s32[]{:S(2)}) async-start(), calls=%async_computation.2 | async-start | bytes 131072 | tf_op jit(solution)/shard_map/psum | solution.py:162
  140.3 181.9 %all-reduce.13.cloned.1.call-start = ((), (), s32[]{:S(2)}) async-start(), calls=%async_computation.3 | async-start | bytes 262144 | tf_op jit(solution)/shard_map/psum | solution.py:162
  248.1 2.1 copy-start.5
  251.5 0.8 copy-start.4
  322.1 2.2 copy-start.3
  325.6 0.8 copy-start.2
Sparse Core Ops, SparseCore 0:
  111.4 28.8 all-reduce.14
  143.2 31.7 all-reduce.16
  178.6 69.4 all-reduce.10
  251.4 70.6 all-reduce.12
